TPU v7x, 512 devices: a whole 4x8x8 slice. The times are simulated.
512 devices in a mesh: rows: 64 (over z, y), feat: 8 (over x, core).
Axes of the slice: x: 4, y: 8, z: 8, core: 2. Of those that a mesh axis runs over, the one named last changes fastest.
Arguments:
- bin_ids: int32 [512, 131072], P('feat', 'rows'), may hold values from 0 to 255
- leaf_ids: int32 [131072], P('rows'), may hold values from 0 to 63
- gradient: float32 [131072], P('rows'), may hold values from -6 to 6
- hessian: float32 [131072], P('rows'), may hold values from 0.01 to 0.25
- raw_feats: bfloat16 [131072, 64], P(('rows', 'feat')), may hold values from -6 to 6
- prior_score: float32 [131072], P(('rows', 'feat')), may hold values from -6 to 6
- elected: int32 [64, 64], P(None, 'feat'), may hold values from 0 to 63, as said below
Outputs:
- relative_gain: float32 [64, 64, 256], P('rows', 'feat')
- coefficients: float32 [64, 65], P('rows')
- new_score: float32 [131072], P(('rows', 'feat'))
Inputs may be any that keep to these rules, and one draw needn't show every extreme that they name: `elected`: within each row, each group's 8 entries are distinct feature numbers of that group.
All inputs are finite; a program needn't handle non-finite values.
Results may differ from a plain program's by a relative error of at most 0.0029.
Values sent between devices are 32-bit elements; how exact they have to be, the bound alone decides.
A program may use at most 64 MiB of HBM per device.

v0:
```python
import jax
import jax.numpy as jnp
from jax import lax
from jax.sharding import PartitionSpec as P

BINS = 256
SPLIT_REG = 1.0
RIDGE_REG = 1.0
SHRINKAGE = 0.3


def split_gains(hist_grad, hist_hess):
    left_grad = jnp.cumsum(hist_grad, axis=-1)
    left_hess = jnp.cumsum(hist_hess, axis=-1)
    total_grad = left_grad[..., -1:]
    total_hess = left_hess[..., -1:]
    right_grad = total_grad - left_grad
    first = left_grad * left_grad / (left_hess + SPLIT_REG)
    second = right_grad * right_grad / (total_hess - left_hess + SPLIT_REG)
    whole = total_grad * total_grad / (total_hess + SPLIT_REG)
    return first + second - whole


def solve_leaves(blocks):
    width = blocks.shape[2]
    system = blocks[:, :width, :] + RIDGE_REG * jnp.eye(width, dtype=blocks.dtype)
    target = blocks[:, width:, :]
    factor = jnp.linalg.cholesky(system)
    middle = lax.linalg.triangular_solve(
        factor, target, left_side=False, lower=True, transpose_a=True
    )
    answer = lax.linalg.triangular_solve(
        factor, middle, left_side=False, lower=True, transpose_a=False
    )
    return -answer[:, 0, :]


def body(bin_ids, leaf_ids, gradient, hessian, raw_feats, prior_score, elected):
    row_total = bin_ids.shape[1]
    leaf_total = elected.shape[0]
    slot_count = elected.shape[1]
    owned = leaf_total // lax.axis_size("rows")
    group_rows = row_total // lax.axis_size("feat")
    grad_round = gradient.astype(jnp.bfloat16)
    hess_round = hessian.astype(jnp.bfloat16)
    zero_value = jnp.zeros((), jnp.bfloat16)
    leaf_table = jnp.arange(leaf_total, dtype=jnp.int32)
    leaf_onehot = (leaf_ids[:, None] == leaf_table[None, :]).astype(jnp.float32)
    elected_cols = jnp.transpose(elected).astype(jnp.float32)
    picked = lax.dot_general(
        elected_cols, leaf_onehot, (((1,), (1,)), ((), ())), precision=lax.Precision.HIGHEST
    ).astype(jnp.int32)
    chosen = jnp.take_along_axis(bin_ids, picked, axis=0)
    bin_table = jnp.arange(BINS, dtype=jnp.int32)
    bin_onehot = (chosen[:, :, None] == bin_table[None, None, :]).astype(jnp.bfloat16)
    wanted = lax.broadcasted_iota(jnp.int32, (1, owned * lax.axis_size("rows")), 1)
    member = leaf_ids[:, None] == wanted
    grad_part = jnp.where(member, grad_round[:, None], zero_value)
    hess_part = jnp.where(member, hess_round[:, None], zero_value)
    weights = jnp.stack([grad_part, hess_part], axis=2).reshape(
        row_total, 2 * (owned * lax.axis_size("rows"))
    )
    product = lax.dot_general(
        weights, bin_onehot, (((0,), (1,)), ((), ())), preferred_element_type=jnp.float32
    )
    histogram = lax.psum_scatter(
        product.reshape(owned * lax.axis_size("rows"), 2, slot_count * BINS),
        "rows",
        scatter_dimension=0,
        tiled=True,
    )
    shaped = histogram.reshape(owned, 2, slot_count, BINS)
    gains = split_gains(shaped[:, 0], shaped[:, 1])
    local_best = jnp.max(gains, axis=(1, 2))
    best = lax.pmax(local_best, "feat")
    relative_gain = gains - best[:, None, None]
    group_start = lax.axis_index("feat") * group_rows
    leaf_sub = lax.dynamic_slice_in_dim(leaf_ids, group_start, group_rows)
    grad_sub = lax.dynamic_slice_in_dim(grad_round, group_start, group_rows)
    hess_sub = lax.dynamic_slice_in_dim(hessian, group_start, group_rows)
    unit_column = jnp.ones((group_rows, 1), jnp.bfloat16)
    augmented = jnp.concatenate([raw_feats, unit_column], axis=1)
    weighted = (hess_sub[:, None] * augmented.astype(jnp.float32)).astype(jnp.bfloat16)
    extended = jnp.concatenate([weighted, grad_sub[:, None]], axis=1)
    ext_width = extended.shape[1]
    wanted = lax.broadcasted_iota(jnp.int32, (1, owned * lax.axis_size("rows")), 1)
    member = leaf_sub[:, None] == wanted
    spread = jnp.where(member[:, :, None], extended[:, None, :], zero_value).reshape(
        group_rows, owned * lax.axis_size("rows") * ext_width
    )
    product = lax.dot_general(
        spread, augmented, (((0,), (0,)), ((), ())), preferred_element_type=jnp.float32
    )
    partial_blocks = lax.psum_scatter(
        product.reshape(owned * lax.axis_size("rows"), ext_width, ext_width - 1),
        "rows",
        scatter_dimension=0,
        tiled=True,
    )
    local_blocks = lax.psum(partial_blocks, "feat")
    coefficients = solve_leaves(local_blocks)
    all_coefs = lax.all_gather(coefficients, "rows", axis=0, tiled=True)
    sub_onehot = (leaf_sub[:, None] == leaf_table[None, :]).astype(jnp.float32)
    row_coefs = jnp.dot(sub_onehot, all_coefs, precision=lax.Precision.HIGHEST)
    new_score = prior_score + SHRINKAGE * jnp.sum(augmented.astype(jnp.float32) * row_coefs, axis=1)
    return (relative_gain, coefficients, new_score)


def solution(mesh):
    in_specs = (
        P("feat", "rows"),
        P("rows"),
        P("rows"),
        P("rows"),
        P(("rows", "feat"), None),
        P(("rows", "feat")),
        P(None, "feat"),
    )
    out_specs = (P("rows", "feat", None), P("rows", None), P(("rows", "feat")))
    return jax.shard_map(body, mesh=mesh, in_specs=in_specs, out_specs=out_specs, check_vma=False)
```

profile of v0, /device:TPU:2, one launch (start us, length us, event | category | flops | bytes accessed | tf_op | source)
XLA Modules:
  0.0 885.3 jit_solution(8825843172253596968)
XLA Ops:
  7.2 0.0 copy-start
  7.2 0.0 all-reduce.6.cloned.1.call-start
  7.2 0.7 convert_element_type.36
  8.0 0.7 convert_element_type.37
  8.7 1.6 compare_select_fusion.2
  10.4 0.0 copy-done
  10.4 0.0 copy-start.2
  10.4 130.6 %gather_fusion = s32[16384]{0:T(1024)S(1)} fusion(s32[64,2048]{1,0:T(8,128)S(1)} %copy-done, s32[16384]{0:T(1024)S(1)} %bitcast.78), kind=kCustom, calls=%fused_computation | custom fusion | bytes 262144 | tf_op jit(solution)/shard_map/jit(take_along_axis)/gather | solution.py:53
  141.0 0.0 copy-done.2
  141.0 0.8 compare_select_fusion.1
  141.8 1.2 pad_maximum_fusion
  143.0 0.2 reshape.597
  143.2 0.3 dot_general.21
  143.6 2.2 iota_compare_fusion
  145.8 0.0 copy-start.1
  145.8 3.0 fusion.3
  148.8 1.8 copy.14
  150.6 0.0 all-reduce.6.cloned.1.call-update
  150.6 0.0 reduce-scatter.4.cloned.1.call-start
  150.7 0.8 dynamic_slice.10
  151.4 0.0 copy-done.1
  151.4 0.1 dynamic_slice.9
  151.5 0.1 dynamic_slice.11
  151.6 0.2 broadcast_select_fusion
  151.8 2.1 select_n.54
  153.9 2.6 dot_general.25
  156.5 0.0 copy-start.5
  156.6 0.0 copy-start.3
  156.6 2.2 fusion.12
  158.7 0.0 reduce-scatter.4.cloned.1.call-update
  158.8 0.0 copy-done.5
  158.8 0.6 fusion.18
  160.0 156.6 %all-reduce.6.cloned.1.call-done = f32[64,2,2048]{2,1,0:T(2,128)} async-done(((f32[64,2,2048]{2,1,0:T(2,128)}), f32[64,2,2048]{2,1,0:T(2,128)}) %all-reduce.6.cloned.1.call-update) | async-done | bytes 1048592
  316.7 1.4 constant_dynamic-slice_fusion
  318.0 0.6 reduce-window.16
  318.6 0.2 slice_reduce_fusion
  318.8 0.6 reduce-window.14
  319.4 0.2 slice_reduce_fusion.1
  319.6 0.1 bitcast_add_fusion.1
  319.6 0.2 slice_reduce_fusion.3
  319.9 0.7 fusion.17
  320.5 10.6 %pmax.7 = f32[]{:T(128)} all-reduce(f32[]{:T(128)} %get-tuple-element.6), channel_id=1, replica_groups=mesh['rows'=64,'feat'=8] {'feat'}, use_global_device_ids=true, to_apply=%region_6.7 | all-reduce | flops 1 | bytes 8 | tf_op jit(solution)/shard_map/pmax | solution.py:75
  331.2 1.2 broadcast_subtract_fusion
  332.4 233.7 %reduce-scatter.4.cloned.1.call-done = f32[1,66,65]{2,1,0:T(8,128)} async-done(((f32[64,66,65]{2,1,0:T(8,128)}), f32[1,66,65]{2,1,0:T(8,128)}) %reduce-scatter.4.cloned.1.call-update) | async-done | bytes 17176
  566.1 21.7 %psum.7 = f32[1,66,65]{2,1,0:T(8,128)S(1)} all-reduce(f32[1,66,65]{2,1,0:T(8,128)} %reduce-scatter.4.cloned.1.call-done), channel_id=1, replica_groups=mesh['rows'=64,'feat'=8] {'feat'}, use_global_device_ids=true, to_apply=%region_8.9 | all-reduce | flops 4290 | bytes 34320 | tf_op jit(solution)/shard_map/psum | solution.py:100
  587.8 0.1 copy.15
  587.9 5.9 custom-call.9
  593.9 0.6 compare_reduce_fusion
  594.6 0.7 fusion.8
  595.2 5.0 custom-call.10
  600.2 0.1 convolution_bitcast_fusion.1
  600.4 0.2 fusion.2
  600.5 0.0 copy-start.4
  600.6 0.3 dynamic-update-slice.3
  600.8 276.6 %all-reduce.1 = f32[4160]{0:T(1024)S(1)} all-reduce(f32[4160]{0:T(1024)S(1)} %dynamic-update-slice.3), channel_id=2, replica_groups=mesh['rows'=64,'feat'=8] {'rows'}, use_global_device_ids=true, to_apply=%add.1 | all-reduce | flops 4160 | bytes 33280
  877.5 0.1 reshape.619
  877.6 0.2 fusion.1
  877.8 0.0 copy-done.3
  877.9 0.6 multiply_add_fusion
  878.4 0.0 copy-done.4
  (18 shorter events, 0.3 us)
Async XLA Ops:
  7.2 3.2 copy-start
  7.2 309.5 %all-reduce.6.cloned.1.call-start = ((), (), s32[]{:S(2)}) async-start(), calls=%async_computation.1 | async-start | bytes 2097152
  10.4 130.6 %copy-start.2 = (s32[2048]{0:T(1024)S(1)}, s32[2048]{0:T(1024)}, u32[]{:S(2)}) copy-start(s32[2048]{0:T(1024)} %param.8) | copy-start | bytes 24580
  145.8 5.7 copy-start.1
  150.6 415.5 %reduce-scatter.4.cloned.1.call-start = ((), (), s32[]{:S(2)}) async-start(), calls=%async_computation.2 | async-start | bytes 2396160
  156.5 2.2 copy-start.5
  156.6 721.3 %copy-start.3 = (f32[256]{0:T(256)S(1)}, f32[256]{0:T(256)}, u32[]{:S(2)}) copy-start(f32[256]{0:T(256)} %param.12) | copy-start | bytes 3076
  600.5 277.9 %copy-start.4 = (f32[65]{0:T(128)}, f32[65]{0:T(128)S(1)}, u32[]{:S(2)}) copy-start(f32[65]{0:T(128)S(1)} %fusion.2) | copy-start | bytes 784
Sparse Core Ops, SparseCore 0:
  150.7 165.8 all-reduce.5
  320.7 245.3 reduce-scatter.3
where the time goes:
time: 886 us; the launch traced here: 885 us
  waiting for transfers between devices  390 us (44%)
  blocking collectives  309 us (35%)
  local copies, waits for them, and re-layouts  141 us (16%)
  other arithmetic  22.2 us (3%)
  between operations  15 us (2%)
    unnamed x4, waiting for transfers between devices  390 us
    unnamed x1, blocking collectives  277 us
    gather x2, local copies, waits for them, and re-layouts, body(): chosen = jnp.take_along_axis(bin_ids, picked, axis=0)  131 us
    psum x1, blocking collectives, body(): local_blocks = lax.psum(partial_blocks, 'feat')  21.7 us
  transfers between devices with their start and end apart: 2, of which 2 were waited for; matrix products, arithmetic and copies ran while one was open for 2% of the time, Pallas kernels for 0%

commit v1 on v0

--- a/solution.py
+++ b/solution.py
@@ -97,7 +97,11 @@
         scatter_dimension=0,
         tiled=True,
     )
-    local_blocks = lax.psum(partial_blocks, "feat")
+    local_blocks = partial_blocks
+    for hop in (1, 2, 4):
+        local_blocks = local_blocks + lax.ppermute(
+            local_blocks, "feat", [(dev, dev ^ hop) for dev in range(8)]
+        )
     coefficients = solve_leaves(local_blocks)
     all_coefs = lax.all_gather(coefficients, "rows", axis=0, tiled=True)
     sub_onehot = (leaf_sub[:, None] == leaf_table[None, :]).astype(jnp.float32)

time: 886 us -> 891 us (level)
  blocking collectives: 309 us -> 289 us
  waiting for transfers between devices: 390 us -> 407 us
    psum x1 -> x0, blocking collectives: 21.7 us -> none  [body(): local_blocks = lax.psum(partial_blocks, 'feat')]
    unnamed x4, waiting for transfers between devices: 390 us -> 403 us
  transfers between devices with their start and end apart: 2 -> 5, of which waited for: 2 -> 4; matrix products, arithmetic and copies ran while one was open for 2% -> 2% of each run, Pallas kernels for 0% -> 0%
where the time goes in v1:
time: 891 us
  waiting for transfers between devices  407 us (46%)
  blocking collectives  289 us (32%)
  local copies, waits for them, and re-layouts  141 us (16%)
  other arithmetic  22.9 us (3%)
  between operations  15 us (2%)
    unnamed x4, waiting for transfers between devices  403 us
    unnamed x1, blocking collectives  277 us
    gather x2, local copies, waits for them, and re-layouts, body(): chosen = jnp.take_along_axis(bin_ids, picked, axis=0)  131 us
  transfers between devices with their start and end apart: 5, of which 4 were waited for; matrix products, arithmetic and copies ran while one was open for 2% of the time, Pallas kernels for 0%

profile of v1, /device:TPU:2, one launch (start us, length us, event | category | flops | bytes accessed | tf_op | source)
XLA Modules:
  0.0 890.8 jit_solution(15174543272794571341)
XLA Ops:
  7.2 0.0 copy-start
  7.2 0.0 all-reduce.6.cloned.1.call-start
  7.2 0.7 convert_element_type.36
  8.0 0.7 convert_element_type.37
  8.7 1.6 compare_select_fusion.2
  10.4 0.0 copy-done
  10.4 0.0 copy-start.2
  10.4 130.6 %gather_fusion = s32[16384]{0:T(1024)S(1)} fusion(s32[64,2048]{1,0:T(8,128)S(1)} %copy-done, s32[16384]{0:T(1024)S(1)} %bitcast.78), kind=kCustom, calls=%fused_computation | custom fusion | bytes 262144 | tf_op jit(solution)/shard_map/jit(take_along_axis)/gather | solution.py:53
  141.0 0.0 copy-done.2
  141.0 0.8 compare_select_fusion.1
  141.8 1.2 pad_maximum_fusion
  143.0 0.2 reshape.597
  143.2 0.3 dot_general.21
  143.6 2.2 iota_compare_fusion
  145.8 0.0 copy-start.1
  145.8 3.0 fusion.3
  148.8 1.8 copy.14
  150.6 0.0 all-reduce.6.cloned.1.call-update
  150.6 0.0 reduce-scatter.4.cloned.1.call-start
  150.7 0.8 dynamic_slice.10
  151.4 0.0 copy-done.1
  151.4 0.1 dynamic_slice.9
  151.5 0.1 dynamic_slice.11
  151.6 0.2 broadcast_select_fusion
  151.8 2.1 select_n.54
  153.9 2.6 dot_general.25
  156.5 0.0 copy-start.5
  156.6 0.0 copy-start.3
  156.6 2.2 fusion.12
  158.7 0.0 reduce-scatter.4.cloned.1.call-update
  158.8 0.0 copy-done.5
  158.8 0.6 fusion.18
  160.0 156.6 %all-reduce.6.cloned.1.call-done = f32[64,2,2048]{2,1,0:T(2,128)} async-done(((f32[64,2,2048]{2,1,0:T(2,128)}), f32[64,2,2048]{2,1,0:T(2,128)}) %all-reduce.6.cloned.1.call-update) | async-done | bytes 1048592
  316.7 1.4 constant_dynamic-slice_fusion
  318.0 0.6 reduce-window.16
  318.6 0.2 slice_reduce_fusion
  318.8 0.6 reduce-window.14
  319.4 0.2 slice_reduce_fusion.1
  319.6 0.1 bitcast_add_fusion.1
  319.6 246.5 %reduce-scatter.4.cloned.1.call-done = f32[1,66,65]{2,1,0:T(8,128)} async-done(((f32[64,66,65]{2,1,0:T(8,128)}), f32[1,66,65]{2,1,0:T(8,128)}) %reduce-scatter.4.cloned.1.call-update) | async-done | bytes 17176
  566.1 1.9 collective-permute-start
  568.1 0.2 slice_reduce_fusion.3
  568.3 1.2 collective-permute-done
  569.4 0.8 add.102
  570.2 2.5 collective-permute-start.1
  572.7 0.7 fusion.17
  573.4 12.6 %pmax.7 = f32[]{:T(128)} all-reduce(f32[]{:T(128)} %get-tuple-element.6), channel_id=1, replica_groups=mesh['rows'=64,'feat'=8] {'feat'}, use_global_device_ids=true, to_apply=%region_6.7 | all-reduce | flops 1 | bytes 8 | tf_op jit(solution)/shard_map/pmax | solution.py:75
  585.9 0.0 collective-permute-done.1
  586.0 3.4 collective-permute-start.2
  589.3 1.2 broadcast_subtract_fusion
  590.6 2.7 collective-permute-done.2
  593.3 0.1 copy.15
  593.5 5.9 custom-call.9
  599.4 0.6 compare_reduce_fusion
  600.1 0.7 fusion.8
  600.7 5.0 custom-call.10
  605.7 0.1 convolution_bitcast_fusion.1
  605.9 0.2 fusion.2
  606.1 0.3 dynamic-update-slice.3
  606.3 276.6 %all-reduce.1 = f32[4160]{0:T(1024)S(1)} all-reduce(f32[4160]{0:T(1024)S(1)} %dynamic-update-slice.3), channel_id=2, replica_groups=mesh['rows'=64,'feat'=8] {'rows'}, use_global_device_ids=true, to_apply=%add.1 | all-reduce | flops 4160 | bytes 33280
  882.9 0.1 reshape.619
  883.1 0.2 fusion.1
  883.3 0.0 copy-done.3
  883.3 0.6 multiply_add_fusion
  (22 shorter events, 0.3 us)
Async XLA Ops:
  7.2 3.2 copy-start
  7.2 309.5 %all-reduce.6.cloned.1.call-start = ((), (), s32[]{:S(2)}) async-start(), calls=%async_computation.1 | async-start | bytes 2097152
  10.4 130.6 %copy-start.2 = (s32[2048]{0:T(1024)S(1)}, s32[2048]{0:T(1024)}, u32[]{:S(2)}) copy-start(s32[2048]{0:T(1024)} %param.8) | copy-start | bytes 24580
  145.8 5.7 copy-start.1
  150.6 415.5 %reduce-scatter.4.cloned.1.call-start = ((), (), s32[]{:S(2)}) async-start(), calls=%async_computation.2 | async-start | bytes 2396160
  156.5 2.2 copy-start.5
  156.6 726.8 %copy-start.3 = (f32[256]{0:T(256)S(1)}, f32[256]{0:T(256)}, u32[]{:S(2)}) copy-start(f32[256]{0:T(256)} %param.12) | copy-start | bytes 3076
  566.1 3.3 collective-permute-start
  570.2 15.7 %collective-permute-start.1 = (f32[1,66,65]{2,1,0:T(8,128)S(1)}, f32[1,66,65]{2,1,0:T(8,128)S(1)}, u32[]{:S(2)}, u32[]{:S(2)}) collective-permute-start(f32[1,66,65]{2,1,0:T(8,128)S(1)} %add.102), channel_id=1, source_target_pairs={{0,2},{1,3},{2,0},{3,1},{4,6},{5,7},{6,4},{7,5},{8,10},{9,11},{10,... | collective-permute-start | bytes 51488 | tf_op jit(solution)/shard_map/ppermute | solution.py:102
  586.0 7.4 collective-permute-start.2
  606.0 277.9 %copy-start.4 = (f32[65]{0:T(128)}, f32[65]{0:T(128)S(1)}, u32[]{:S(2)}) copy-start(f32[65]{0:T(128)S(1)} %fusion.2) | copy-start | bytes 784
Sparse Core Ops, SparseCore 0:
  150.7 165.8 all-reduce.5
  320.7 245.3 reduce-scatter.3
